TPU v7x, 32 devices: a whole 2x2x4 slice. The times are simulated.
32 devices in a mesh: row: 8 (over y, x, core), col: 4 (over z).
Axes of the slice: x: 2, y: 2, z: 4, core: 2. Of those that a mesh axis runs over, the one named last changes fastest.
Arguments:
- tokens: bfloat16 [1024, 12288], P('row', 'col'), may hold values from -10 to 10
- qkv_weight: bfloat16 [12288, 3, 8192], P('col', None, 'row'), as said below
- out_weight: bfloat16 [8192, 12288], P('row', 'col'), may hold values from -0.0625 to 0.0625
Outputs:
- mixed: bfloat16 [1024, 12288], P('row', 'col')
Inputs may be any that keep to these rules, and one draw needn't show every extreme that they name: `qkv_weight`: entries of magnitude at most 3 / sqrt(12288).
All inputs are finite; a program needn't handle non-finite values.
Results may differ from a plain program's by a relative error of at most 0.0055.
Values may be sent and summed in bfloat16 or wider, within the bound.
A program may use at most 128 MiB of HBM per device.

v0:
```python
from functools import partial
import math

import jax
import jax.numpy as jnp
from jax import lax
from jax.sharding import PartitionSpec as P

HD = 128


def attend(state, pieces, offset, query_heads, query_first):
    key_rows, value_rows = pieces
    number = key_rows.shape[0]
    head_count = query_heads.shape[1]
    key_heads = key_rows.reshape(number, head_count, HD)
    value_heads = value_rows.reshape(number, head_count, HD)
    top_old, total_old, accum_old = state
    scores = jnp.einsum("qhd,khd->qhk", query_heads, key_heads, preferred_element_type=jnp.float32)
    scores = scores * (1.0 / math.sqrt(HD))
    query_pos = query_first + jnp.arange(query_heads.shape[0], dtype=jnp.int32)
    key_pos = jnp.arange(number, dtype=jnp.int32)
    causal = (query_pos[:, None] >= key_pos[None, :])[:, None, :]
    scores = jnp.where(causal, scores, -1e30)
    top_new = jnp.maximum(top_old, jnp.max(scores, axis=2))
    weights = jnp.where(causal, jnp.exp(scores - top_new[:, :, None]), 0.0)
    total_new = jnp.sum(weights, axis=2)
    update = jnp.einsum(
        "qhk,khd->qhd",
        weights.astype(jnp.bfloat16),
        value_heads,
        preferred_element_type=jnp.float32,
    )
    return (top_new, total_new, update)


def local(tokens, qkv_weight, out_weight):
    panel_rows = lax.all_gather(tokens, "row", axis=0, tiled=True)
    model_cols = panel_rows.shape[1]
    head_cols = qkv_weight.shape[2]
    weight_flat = qkv_weight.reshape(model_cols, 3 * head_cols)
    query_count = panel_rows.shape[0] // lax.axis_size("col")
    query_first = lax.axis_index("col") * query_count
    head_count = head_cols // HD
    state_init = (
        jnp.full((query_count, head_count), -1e30, jnp.float32),
        jnp.zeros((query_count, head_count), jnp.float32),
        jnp.zeros((query_count, head_count, HD), jnp.float32),
    )
    block = panel_rows
    projected = lax.psum_scatter(
        jnp.dot(block, weight_flat, preferred_element_type=jnp.float32),
        "col",
        scatter_dimension=0,
        tiled=True,
    ).astype(jnp.bfloat16)
    query_heads = projected[:, :head_cols].reshape(query_count, head_count, HD)
    key_rows = projected[:, head_cols : 2 * head_cols]
    value_rows = projected[:, 2 * head_cols :]
    folder = partial(attend, query_heads=query_heads, query_first=query_first)
    final = folder(
        state_init,
        (
            lax.all_gather(key_rows, "col", axis=0, tiled=True),
            lax.all_gather(value_rows, "col", axis=0, tiled=True),
        ),
        jnp.int32(0),
    )
    context = (final[2] / final[1][:, :, None]).reshape(query_count, head_cols).astype(jnp.bfloat16)
    gathered = lax.all_gather(context, "col", axis=0, tiled=True)
    block = gathered
    summed = lax.psum_scatter(
        jnp.dot(block, out_weight, preferred_element_type=jnp.float32),
        "row",
        scatter_dimension=0,
        tiled=True,
    )
    return (tokens.astype(jnp.float32) + summed).astype(jnp.bfloat16)


def solution(mesh):
    in_specs = (P("row", "col"), P("col", None, "row"), P("row", "col"))
    out_specs = P("row", "col")
    return jax.shard_map(local, mesh=mesh, in_specs=in_specs, out_specs=out_specs, check_vma=False)
```

profile of v0, /device:TPU:0, one launch (start us, length us, event | category | flops | bytes accessed | tf_op | source)
XLA Modules:
  0.0 558.3 jit_solution(12852301343964477909)
XLA Ops:
  6.5 0.0 all-gather.5.cloned.1.call-start
  6.5 0.7 all-gather.5.cloned.1.call-update
  7.3 0.0 reduce-scatter.3.cloned.1.call-start
  7.3 24.8 %copy.8 = bf16[3072,3,1024]{0,2,1:T(8,128)(2,1)} copy(bf16[3072,3,1024]{2,0,1:T(8,128)(2,1)} %param.4) | data formatting | bytes 37748736 | tf_op args[1]
  32.1 25.3 %all-gather.5.cloned.1.call-done = bf16[1024,3072]{1,0:T(8,128)(2,1)} async-done(((bf16[128,3072]{1,0:T(8,128)(2,1)}), bf16[1024,3072]{1,0:T(8,128)(2,1)}) %all-gather.5.cloned.1.call-update) | async-done | bytes 6291472 | tf_op jit(solution)/shard_map/all_gather | solution.py:38
  57.4 26.3 %fusion.19 = f32[1024,3072]{1,0:T(8,128)} fusion(bf16[1024,3072]{1,0:T(8,128)(2,1)} %all-gather.5.cloned.1.call-done, bf16[3072,3072]{0,1:T(8,128)(2,1)} %bitcast.43), kind=kOutput, calls=%fused_computation.22 | convolution fusion | flops 19327352832 | bytes 37748736 | tf_op jit(solution)/shard_map/dot_general | solution.py:52
  83.7 0.0 reduce-scatter.3.cloned.1.call-update
  83.7 0.0 all-gather.9.cloned.1.call-start
  83.7 212.0 %reduce-scatter.3.cloned.1.call-done = f32[256,3072]{1,0:T(8,128)} async-done(((f32[1024,3072]{1,0:T(8,128)}), f32[256,3072]{1,0:T(8,128)}) %reduce-scatter.3.cloned.1.call-update) | async-done | bytes 3145744 | tf_op jit(solution)/shard_map/reduce_scatter | solution.py:51
  295.7 2.1 convert_element_type.19
  297.8 1.1 slice_bitcast_fusion
  298.9 0.0 all-gather.9.cloned.1.call-update
  299.0 0.0 all-gather.7.cloned.1.call-start
  299.0 0.5 all-gather.7.cloned.1.call-update
  299.5 0.0 all-gather.11.cloned.1.call-start
  299.6 0.2 iota_compare_fusion
  299.8 46.0 %all-gather.9.cloned.1.call-done = bf16[1024,1024]{1,0:T(8,128)(2,1)} async-done(((bf16[256,1024]{1,0:T(8,128)(2,1)}), bf16[1024,1024]{1,0:T(8,128)(2,1)}) %all-gather.9.cloned.1.call-update) | async-done | bytes 2097168 | tf_op jit(solution)/shard_map/all_gather | solution.py:64
  345.8 3.2 fusion
  349.0 0.0 copy-start
  349.0 3.2 copy-done
  352.2 2.0 fusion.1
  354.2 37.5 %all-gather.7.cloned.1.call-done = bf16[1024,1024]{1,0:T(8,128)(2,1)} async-done(((bf16[256,1024]{1,0:T(8,128)(2,1)}), bf16[1024,1024]{1,0:T(8,128)(2,1)}) %all-gather.7.cloned.1.call-update) | async-done | bytes 2097168 | tf_op jit(solution)/shard_map/all_gather | solution.py:65
  391.7 2.9 copy.14
  394.6 6.4 %divide_convert_fusion = bf16[256,8,128]{0,2,1:T(8,128)(2,1)} fusion(bf16[1024,8,128]{0,2,1:T(8,128)(2,1)S(1)} %bitcast.44, f32[8,1024,256]{2,1,0:T(8,128)} %copy-done, f32[256,8]{0,1:T(8,128)S(1)} %broadcast_maximum_fusion, pred[256,1024]{0,1:T(8,128)(4,1)S(1)} %iota_compare_fusion, f32[256,8]{0,1:T(8,128)S(1)} %fusion.1), kind=kOutput, calls=%fused_computation.12 | convolution fusion | flops 547880960 | bytes 11288576 | tf_op jit(solution)/shard_map/qhk,khd->qhd/dot_general | solution.py:28
  401.0 0.0 all-gather.11.cloned.1.call-update
  401.0 0.2 reduce-scatter.5.cloned.1.call-start
  401.2 45.0 %all-gather.11.cloned.1.call-done = bf16[1024,1024]{0,1:T(8,128)(2,1)} async-done(((bf16[256,1024]{0,1:T(8,128)(2,1)}), bf16[1024,1024]{0,1:T(8,128)(2,1)}) %all-gather.11.cloned.1.call-update) | async-done | bytes 2097168 | tf_op jit(solution)/shard_map/all_gather | solution.py:70
  446.2 12.2 %fusion.20 = f32[1024,3072]{1,0:T(8,128)} fusion(bf16[1024,1024]{0,1:T(8,128)(2,1)} %all-gather.11.cloned.1.call-done, bf16[1024,3072]{1,0:T(8,128)(2,1)} %param.5), kind=kOutput, calls=%fused_computation.23 | convolution fusion | flops 6442450944 | bytes 20971520 | tf_op jit(solution)/shard_map/dot_general | solution.py:73
  458.4 0.0 copy-start.1
  458.4 0.0 reduce-scatter.5.cloned.1.call-update
  458.4 90.6 %reduce-scatter.5.cloned.1.call-done = f32[128,3072]{1,0:T(8,128)} async-done(((f32[1024,3072]{1,0:T(8,128)}), f32[128,3072]{1,0:T(8,128)}) %reduce-scatter.5.cloned.1.call-update) | async-done | bytes 1572880 | tf_op jit(solution)/shard_map/reduce_scatter | solution.py:72
  549.0 0.0 copy-done.1
  549.0 2.4 add_convert_fusion
  (2 shorter events, 0.0 us)
Async XLA Ops:
  6.5 50.8 %all-gather.5.cloned.1.call-start = ((), (), s32[]{:S(2)}) async-start(), calls=%async_computation.2 | async-start | bytes 7077888 | tf_op jit(solution)/shard_map/all_gather | solution.py:38
  7.3 288.5 %reduce-scatter.3.cloned.1.call-start = ((), (), s32[]{:S(2)}) async-start(), calls=%async_computation.3 | async-start | bytes 15728640 | tf_op jit(solution)/shard_map/reduce_scatter | solution.py:51
  83.7 262.1 %all-gather.9.cloned.1.call-start = ((), (), s32[]{:S(2)}) async-start(), calls=%async_computation.5 | async-start | bytes 2621440 | tf_op jit(solution)/shard_map/all_gather | solution.py:64
  299.0 92.8 %all-gather.7.cloned.1.call-start = ((), (), s32[]{:S(2)}) async-start(), calls=%async_computation.4 | async-start | bytes 2621440 | tf_op jit(solution)/shard_map/all_gather | solution.py:65
  299.5 146.7 %all-gather.11.cloned.1.call-start = ((), (), s32[]{:S(2)}) async-start(), calls=%async_computation.6 | async-start | bytes 2621440 | tf_op jit(solution)/shard_map/all_gather | solution.py:70
  349.0 3.2 copy-start
  401.0 148.0 %reduce-scatter.5.cloned.1.call-start = ((), (), s32[]{:S(2)}) async-start(), calls=%async_computation.7 | async-start | bytes 14155776 | tf_op jit(solution)/shard_map/reduce_scatter | solution.py:72
  458.4 90.6 %copy-start.1 = (bf16[128,3072]{1,0:T(8,128)(2,1)S(1)}, bf16[128,3072]{1,0:T(8,128)(2,1)}, u32[]{:S(2)}) copy-start(bf16[128,3072]{1,0:T(8,128)(2,1)} %param.3) | copy-start | bytes 2359300
Sparse Core Ops, SparseCore 0:
  9.2 48.1 all-gather.4
  83.8 211.8 reduce-scatter.2
  299.1 46.6 all-gather.8
  347.2 44.4 all-gather.6
  401.1 45.0 all-gather.10
  458.6 90.4 reduce-scatter.4
where the time goes:
time: 559 us; the launch traced here: 558 us
  waiting for transfers between devices  458 us (82%)
  matrix products  48 us (9%)
  local copies, waits for them, and re-layouts  31.9 us (6%)
  between operations  13.5 us (2%)
  other arithmetic  6.71 us (1%)
    reduce_scatter x1, waiting for transfers between devices, local(): lax.psum_scatter(jnp.dot(block, weight_flat, preferred_element_type=jnp.f...  212 us
    reduce_scatter x1, waiting for transfers between devices, local(): lax.psum_scatter(jnp.dot(block, out_weight, preferred_element_type=jnp.fl...  90.6 us
    all_gather x1, waiting for transfers between devices, local(): lax.all_gather(key_rows, 'col', axis=0, tiled=True)  46 us
    all_gather x1, waiting for transfers between devices, local(): gathered = lax.all_gather(context, 'col', axis=0, tiled=True)  45 us
    all_gather x1, waiting for transfers between devices, local(): lax.all_gather(value_rows, 'col', axis=0, tiled=True)  37.5 us
    unnamed x6, local copies, waits for them, and re-layouts  29.1 us
    dot_general x1, matrix products, local(): jnp.dot(block, weight_flat, preferred_element_type=jnp.float32)  26.3 us
    all_gather x1, waiting for transfers between devices, local(): panel_rows = lax.all_gather(tokens, 'row', axis=0, tiled=True)  25.3 us
  transfers between devices with their start and end apart: 6, of which 6 were waited for; matrix products, arithmetic and copies ran while one was open for 5% of the time, Pallas kernels for 0%

commit v1 on v0

v1 whole, which is shorter than its diff:
```python
from functools import partial
import math

import jax
import jax.numpy as jnp
from jax import lax
from jax.experimental import pallas as pl
from jax.experimental.pallas import tpu as pltpu
from jax.sharding import PartitionSpec as P

HD = 128


def attend_block(q, k, v, first):
    scores = lax.dot_general(q, k, (((1,), (1,)), ((), ())), preferred_element_type=jnp.float32)
    scores = scores * (1.0 / math.sqrt(HD))
    row = lax.broadcasted_iota(jnp.int32, scores.shape, 0) + first
    col = lax.broadcasted_iota(jnp.int32, scores.shape, 1)
    causal = row >= col
    scores = jnp.where(causal, scores, -1e30)
    top = jnp.max(scores, axis=1, keepdims=True)
    weights = jnp.where(causal, jnp.exp(scores - top), 0.0)
    total = jnp.sum(weights, axis=1, keepdims=True)
    update = jnp.dot(weights.astype(jnp.bfloat16), v, preferred_element_type=jnp.float32)
    return (update / total).astype(jnp.bfloat16)


MESH = pl.DeviceIdType.MESH
SKEW = 2
GROUPS = 2


def fused_kernel(n, ranks, tok_ref, w_ref, ow_ref, out_ref, panel, wv, ow, acc, send, recv, final, ctx, swap, arrived, resid,
                 w_sem, own_sem, ts, fs, tr, rs_s, rs_r, cx_s, cx_r, sw_s, sw_r, rw_s, rw_r):
    groups = GROUPS
    tb, depth = tok_ref.shape
    half = w_ref.shape[2] // 2
    wg = half // groups
    chips = ranks // 2
    number = tb * ranks
    pieces = ranks * groups
    blocks = cx_s.shape[2]
    qb = number // blocks
    r = lax.axis_index("row")
    z = lax.axis_index("col")
    core = lax.rem(r, 2)
    chip = r // 2
    cx = lax.rem(chip, 2)
    cy = chip // 2
    partner = chip * 2 + 1 - core

    def peer(p, c):
        px = lax.rem(cx + lax.rem(p, 2), 2)
        py = lax.rem(cy + p // 2, chips // 2)
        return (py * 2 + px) * 2 + lax.rem(core + c, 2)

    def w_copy(d, g, s):
        first = d * half + g * wg
        return pltpu.make_async_copy(w_ref.at[s, :, pl.ds(first, wg)], wv.at[d, g, s], w_sem.at[d, g, s])

    own = pltpu.make_async_copy(tok_ref, panel.at[r], own_sem.at[0])
    own.start()
    for g in range(groups):
        for d in range(2):
            for s in range(3):
                w_copy(d, g, s).start()
    ow_copy = pltpu.make_async_copy(ow_ref, ow, own_sem.at[1])
    ow_copy.start()
    resid_copy = pltpu.make_async_copy(tok_ref, resid, own_sem.at[2])
    resid_copy.start()

    barrier = pltpu.get_barrier_semaphore()
    pl.semaphore_signal(barrier, inc=1, device_id={"row": partner}, device_id_type=MESH)
    for p in range(1, chips):
        pl.semaphore_signal(barrier, inc=1, device_id={"row": peer(p, 0)}, device_id_type=MESH)

    @pl.when(z > 0)
    def _():
        pl.semaphore_signal(barrier, inc=1, device_id={"col": z - 1}, device_id_type=MESH)

    @pl.when(z < n - 1)
    def _():
        pl.semaphore_signal(barrier, inc=1, device_id={"col": z + 1}, device_id_type=MESH)

    pl.semaphore_wait(barrier, chips + jnp.where(z > 0, 1, 0) + jnp.where(z < n - 1, 1, 0))

    def tok_send(p):
        target = partner if p == 0 else peer(p, 0)
        return pltpu.make_async_remote_copy(
            tok_ref, panel.at[r], ts.at[p], tr.at[r], device_id={"row": target}, device_id_type=MESH)

    def tok_forward(p):
        block = panel.at[peer(p, 0)]
        return pltpu.make_async_remote_copy(
            block, block, fs.at[p], tr.at[peer(p, 0)], device_id={"row": partner}, device_id_type=MESH)

    def tok_wait(source):
        block = panel.at[source]
        pltpu.make_async_remote_copy(
            block, block, fs.at[0], tr.at[source], device_id={"row": partner}, device_id_type=MESH).wait_recv()

    early = min(3, chips)
    for p in range(early):
        tok_send(p).start()

    def decode(k):
        lead = 2 * groups
        each = 2 * (chips - 1)
        j = jnp.maximum(k - lead, 0)
        p = jnp.where(k < lead, 0, 1 + lax.rem(j, each) // 2)
        g = jnp.where(k < lead, k // 2, j // each)
        return p, g, lax.rem(k, 2)

    def rs_copy(d, k):
        target = jnp.maximum(z - 1, 0) if d == 0 else jnp.minimum(z + 1, n - 1)
        return pltpu.make_async_remote_copy(
            send.at[d, k], recv.at[d, k], rs_s.at[d, k], rs_r.at[d, k],
            device_id={"col": target}, device_id_type=MESH)

    def work(d, k):
        p, g, c = decode(k)
        source = peer(p, c)
        is_source = (z == n - 1) if d == 0 else (z == 0)
        is_sink = (z == 0) if d == 0 else (z == n - 1)

        @pl.when(k < 2 * groups)
        def _():
            @pl.when(lax.rem(k, 2) == 0)
            def _():
                for s in range(3):
                    pltpu.make_async_copy(
                        w_ref.at[s, :, pl.ds(0, wg)], wv.at[d, g, s], w_sem.at[d, g, s]).wait()

        for s in range(3):
            acc[d, s] = jnp.dot(panel[source], wv[d, g, s], preferred_element_type=jnp.float32)

        @pl.when(jnp.logical_not(is_source))
        def _():
            rs_copy(d, k).wait_recv()

        @pl.when(is_source)
        def _():
            for s in range(3):
                send[d, k, s] = acc[d, s].astype(jnp.bfloat16)

        @pl.when(jnp.logical_not(jnp.logical_or(is_source, is_sink)))
        def _():
            for s in range(3):
                send[d, k, s] = (acc[d, s] + recv[d, k, s].astype(jnp.float32)).astype(jnp.bfloat16)

        @pl.when(is_sink)
        def _():
            rows = pl.ds(pl.multiple_of(source * tb, tb), tb)
            for s in range(3):
                final[g, s, rows, :] = (acc[d, s] + recv[d, k, s].astype(jnp.float32)).astype(jnp.bfloat16)

        @pl.when(jnp.logical_not(is_sink))
        def _():
            rs_copy(d, k).start()

    def step(i, carry):
        @pl.when(i < pieces)
        def _():
            p, g, c = decode(i)

            @pl.when(g == 0)
            def _():
                @pl.when(i == 0)
                def _():
                    own.wait()

                @pl.when(i > 0)
                def _():
                    tok_wait(peer(p, c))

                @pl.when(jnp.logical_and(p > 0, c == 0))
                def _():
                    tok_forward(p).start()

        if chips > early:
            @pl.when(i == 2)
            def _():
                for p in range(early, chips):
                    tok_send(p).start()

        for d in range(2):
            k = i - SKEW * ((n - 1 - z) if d == 0 else z)

            @pl.when(jnp.logical_and(k >= 0, k < pieces))
            def _():
                work(d, k)

        return carry

    lax.fori_loop(0, pieces + SKEW * (n - 1), step, 0)

    def ctx_copy(e, g, b):
        target = jnp.minimum(z + 1, n - 1) if e == 0 else jnp.maximum(z - 1, 0)
        part = ctx.at[e, g, pl.ds(b * qb, qb), :]
        return pltpu.make_async_remote_copy(
            part, part, cx_s.at[e, g, b], cx_r.at[e, g, b], device_id={"col": target}, device_id_type=MESH)

    for e in range(2):
        @pl.when(z == (0 if e == 0 else n - 1))
        def _():
            def group(g, carry):
                for b in range(blocks):
                    first, last = b * qb, (b + 1) * qb
                    for h in range(0, wg, HD):
                        ctx[e, g, first:last, h : h + HD] = attend_block(
                            final[g, 0, first:last, h : h + HD], final[g, 1, :last, h : h + HD],
                            final[g, 2, :last, h : h + HD], first)
                    ctx_copy(e, g, b).start()
                return carry

            lax.fori_loop(0, groups, group, 0)

    def relay(i, carry):
        g, b = i // blocks, lax.rem(i, blocks)
        for e in range(2):
            @pl.when(z != (0 if e == 0 else n - 1))
            def _():
                ctx_copy(e, g, b).wait_recv()

                @pl.when(z != (n - 1 if e == 0 else 0))
                def _():
                    ctx_copy(e, g, b).start()

        return carry

    lax.fori_loop(0, groups * blocks, relay, 0)
    for p in range(1, chips):
        tok_forward(p).wait_send()
    ow_copy.wait()
    wide = ow.shape[1] // 4

    def swap_copy(p):
        return pltpu.make_async_remote_copy(
            panel.at[peer(p, 1)], swap.at[p], sw_s.at[p], sw_r.at[p],
            device_id={"row": partner}, device_id_type=MESH)

    def row_copy(p):
        return pltpu.make_async_remote_copy(
            panel.at[peer(p, 0)], arrived.at[chip], rw_s.at[p], rw_r.at[chip],
            device_id={"row": peer(p, 0)}, device_id_type=MESH)

    def row_wait(p):
        source = peer(p, 0)
        pltpu.make_async_remote_copy(
            arrived.at[source // 2], arrived.at[source // 2], rw_s.at[p], rw_r.at[source // 2],
            device_id={"row": source}, device_id_type=MESH).wait_recv()

    def out_step(t, carry):
        @pl.when(t < chips)
        def _():
            p = chips - 1 - t
            pair = peer(p, 0) // 2
            rows = pl.ds(pl.multiple_of(pair * 2 * tb, 2 * tb), 2 * tb)

            def tile(i, carry):
                cols = pl.ds(pl.multiple_of(i * wide, 128), wide)
                total = jnp.zeros((2 * tb, wide), jnp.float32)
                for e in range(2):
                    for g in range(groups):
                        first = e * half + g * wg
                        total += jnp.dot(ctx[e, g, rows, :], ow[first : first + wg, cols], preferred_element_type=jnp.float32)
                panel[pair * 2, :, cols] = total[:tb].astype(jnp.bfloat16)
                panel[pair * 2 + 1, :, cols] = total[tb:].astype(jnp.bfloat16)
                return carry

            lax.fori_loop(0, 4, tile, 0)
            swap_copy(p).start()

        @pl.when(t >= 1)
        def _():
            p = chips - t
            swap_copy(p).wait_recv()
            mine = peer(p, 0)

            def tile(i, carry):
                cols = pl.ds(pl.multiple_of(i * wide, 128), wide)
                panel[mine, :, cols] = (
                    panel[mine, :, cols].astype(jnp.float32) + swap[p, :, cols].astype(jnp.float32)
                ).astype(jnp.bfloat16)
                return carry

            lax.fori_loop(0, 4, tile, 0)

            @pl.when(p > 0)
            def _():
                row_copy(p).start()

        return carry

    lax.fori_loop(0, chips + 1, out_step, 0)
    resid_copy.wait()
    for p in range(1, chips):
        row_wait(p)

    def finish(i, carry):
        cols = pl.ds(pl.multiple_of(i * wide, 128), wide)
        total = panel[r, :, cols].astype(jnp.float32)
        for p in range(1, chips):
            total += arrived[peer(p, 0) // 2, :, cols].astype(jnp.float32)
        out_ref[:, cols] = (resid[:, cols].astype(jnp.float32) + total).astype(jnp.bfloat16)
        return carry

    lax.fori_loop(0, 4, finish, 0)

    for p in range(chips):
        tok_send(p).wait_send()
        swap_copy(p).wait_send()
    for p in range(1, chips):
        row_copy(p).wait_send()

    def drain(k, carry):
        for d in range(2):
            @pl.when(z != (0 if d == 0 else n - 1))
            def _():
                rs_copy(d, k).wait_send()
        return carry

    lax.fori_loop(0, pieces, drain, 0)

    def drain_ctx(i, carry):
        g, b = i // blocks, lax.rem(i, blocks)
        for e in range(2):
            @pl.when(z != (n - 1 if e == 0 else 0))
            def _():
                ctx_copy(e, g, b).wait_send()
        return carry

    lax.fori_loop(0, groups * blocks, drain_ctx, 0)


def fused_local(tokens, qkv_weight, out_weight):
    n, ranks = lax.axis_size("col"), lax.axis_size("row")
    tb, depth = tokens.shape
    cols = qkv_weight.shape[2]
    wg = cols // 2 // GROUPS
    number = tb * ranks
    pieces = ranks * GROUPS
    blocks = max(1, number // 256)
    planes = jnp.transpose(qkv_weight, (1, 0, 2))
    bf16, f32, dma = jnp.bfloat16, jnp.float32, pltpu.SemaphoreType.DMA
    return pl.pallas_call(
        partial(fused_kernel, n, ranks),
        in_specs=[pl.BlockSpec(memory_space=pl.ANY)] * 3,
        out_specs=pl.BlockSpec(memory_space=pltpu.VMEM),
        out_shape=jax.ShapeDtypeStruct(tokens.shape, bf16),
        scratch_shapes=[
            pltpu.VMEM((ranks, tb, depth), bf16),
            pltpu.VMEM((2, GROUPS, 3, depth, wg), bf16),
            pltpu.VMEM(out_weight.shape, bf16),
            pltpu.VMEM((2, 3, tb, wg), f32),
            pltpu.VMEM((2, pieces, 3, tb, wg), bf16),
            pltpu.VMEM((2, pieces, 3, tb, wg), bf16),
            pltpu.VMEM((GROUPS, 3, number, wg), bf16),
            pltpu.VMEM((2, GROUPS, number, wg), bf16),
            pltpu.VMEM((ranks // 2, tb, depth), bf16),
            pltpu.VMEM((ranks // 2, tb, depth), bf16),
            pltpu.VMEM((tb, depth), bf16),
            dma((2, GROUPS, 3)), dma((3,)), dma((ranks // 2,)), dma((ranks // 2,)), dma((ranks,)),
            dma((2, pieces)), dma((2, pieces)), dma((2, GROUPS, blocks)), dma((2, GROUPS, blocks)),
            dma((ranks // 2,)), dma((ranks // 2,)), dma((ranks // 2,)), dma((ranks // 2,)),
        ],
        compiler_params=pltpu.CompilerParams(
            collective_id=0, has_side_effects=True, vmem_limit_bytes=67043328),
    )(tokens, planes, out_weight)

def tokens_local(tokens, qkv_weight, out_weight):
    n = lax.axis_size("col")
    panel = lax.all_gather(tokens, "row", axis=0, tiled=True)
    depth, _, head_cols = qkv_weight.shape
    count = panel.shape[0] // n
    first = lax.axis_index("col") * count
    heads = head_cols // HD
    product = jnp.dot(panel, qkv_weight.reshape(depth, 3 * head_cols), preferred_element_type=jnp.float32)
    qkv = lax.psum_scatter(product, "col", scatter_dimension=0, tiled=True).astype(jnp.bfloat16)
    q = qkv[:, :head_cols].reshape(count, heads, HD)
    k = lax.all_gather(qkv[:, head_cols : 2 * head_cols], "col", axis=0, tiled=True).reshape(-1, heads, HD)
    v = lax.all_gather(qkv[:, 2 * head_cols :], "col", axis=0, tiled=True).reshape(-1, heads, HD)
    scores = jnp.einsum("qhd,khd->qhk", q, k, preferred_element_type=jnp.float32) * (1.0 / math.sqrt(HD))
    causal = (first + jnp.arange(count)[:, None] >= jnp.arange(k.shape[0])[None, :])[:, None, :]
    scores = jnp.where(causal, scores, -1e30)
    weights = jnp.where(causal, jnp.exp(scores - jnp.max(scores, axis=2, keepdims=True)), 0.0)
    total = jnp.sum(weights, axis=2)
    update = jnp.einsum("qhk,khd->qhd", weights.astype(jnp.bfloat16), v, preferred_element_type=jnp.float32)
    context = (update / total[:, :, None]).reshape(count, head_cols).astype(jnp.bfloat16)
    gathered = lax.all_gather(context, "col", axis=0, tiled=True)
    product = jnp.dot(gathered, out_weight, preferred_element_type=jnp.float32)
    summed = lax.psum_scatter(product, "row", scatter_dimension=0, tiled=True)
    return (tokens.astype(jnp.float32) + summed).astype(jnp.bfloat16)


def local(tokens, qkv_weight, out_weight):
    ranks, width = lax.axis_size("row"), qkv_weight.shape[2]
    if ranks % 4 == 0 and lax.axis_size("col") > 1 and width % (2 * GROUPS * HD) == 0:
        return fused_local(tokens, qkv_weight, out_weight)
    return tokens_local(tokens, qkv_weight, out_weight)


def solution(mesh):
    in_specs = (P("row", "col"), P("col", None, "row"), P("row", "col"))
    out_specs = P("row", "col")
    return jax.shard_map(local, mesh=mesh, in_specs=in_specs, out_specs=out_specs, check_vma=False)
```

time: 559 us -> 215 us (0.38)
  waiting for transfers between devices: 458 us -> 0 us
  Pallas kernels: 0 us -> 213 us
  matrix products: 48 us -> 0 us
  local copies, waits for them, and re-layouts: 31.9 us -> 2.06 us
  between operations: 13.5 us -> 0.01 us
  other arithmetic: 6.71 us -> 0 us
    reduce_scatter x2 -> x0, waiting for transfers between devices: 303 us -> none  [the longest x1 212 us: local(): lax.psum_scatter(jnp.dot(block, weight_flat, preferred_element_type=jnp.f...]
    pallas_call x0 -> x1, Pallas kernels: none -> 213 us  [fused_local(): pl.pallas_call(partial(fused_kernel, n, ranks), in_specs=[pl.BlockSpec(me...]
    all_gather x4 -> x0, waiting for transfers between devices: 154 us -> none  [the longest x1 46 us: local(): lax.all_gather(key_rows, 'col', axis=0, tiled=True)]
    dot_general x4 -> x0, matrix products: 48 us -> none  [the longest x1 26.3 us: local(): jnp.dot(block, weight_flat, preferred_element_type=jnp.float32)]
    unnamed x6 -> x1, local copies, waits for them, and re-layouts: 29.1 us -> 2.06 us
  transfers between devices with their start and end apart: 6 -> 0, of which waited for: 6 -> 0; matrix products, arithmetic and copies ran while one was open for 5% -> 0% of each run, Pallas kernels for 0% -> 0%
where the time goes in v1:
time: 215 us
  Pallas kernels  213 us (99%)
    pallas_call x1, Pallas kernels, fused_local(): pl.pallas_call(partial(fused_kernel, n, ranks), in_specs=[pl.BlockSpec(me...  213 us

profile of v1, /device:TPU:0, one launch (start us, length us, event | category | flops | bytes accessed | tf_op | source)
XLA Modules:
  0.0 214.7 jit_solution(7022925857896033961)
XLA Ops:
  0.0 212.6 %shard_map.37 = bf16[128,3072]{1,0:T(8,128)(2,1)} custom-call(bf16[128,3072]{1,0:T(8,128)(2,1)} %tok_ref.1, bf16[3,3072,1024]{2,1,0:T(8,128)(2,1)} %bitcast.1, bf16[1024,3072]{1,0:T(8,128)(2,1)} %ow_ref.1), custom_call_target="tpu_custom_call" | custom-call | tf_op jit(solution)/shard_map/pallas_call | solution.py:346
  212.6 2.1 copy.5

commit v2 on v1

--- a/solution.py
+++ b/solution.py
@@ -158,6 +158,22 @@
         def _():
             rs_copy(d, k).start()
 
+    def ctx_copy(e, g, b):
+        target = jnp.minimum(z + 1, n - 1) if e == 0 else jnp.maximum(z - 1, 0)
+        part = ctx.at[e, g, pl.ds(b * qb, qb), :]
+        return pltpu.make_async_remote_copy(
+            part, part, cx_s.at[e, g, b], cx_r.at[e, g, b], device_id={"col": target}, device_id_type=MESH)
+
+    def attend(e, g, b):
+        first, last = b * qb, (b + 1) * qb
+        for h in range(0, wg, HD):
+            ctx[e, g, first:last, h : h + HD] = attend_block(
+                final[g, 0, first:last, h : h + HD], final[g, 1, :last, h : h + HD],
+                final[g, 2, :last, h : h + HD], first)
+        ctx_copy(e, g, b).start()
+
+    ready = 2 * groups + 2 * (chips - 1) + SKEW * (n - 1)
+
     def step(i, carry):
         @pl.when(i < pieces)
         def _():
@@ -190,30 +206,27 @@
             def _():
                 work(d, k)
 
-        return carry
-
-    lax.fori_loop(0, pieces + SKEW * (n - 1), step, 0)
-
-    def ctx_copy(e, g, b):
-        target = jnp.minimum(z + 1, n - 1) if e == 0 else jnp.maximum(z - 1, 0)
-        part = ctx.at[e, g, pl.ds(b * qb, qb), :]
-        return pltpu.make_async_remote_copy(
-            part, part, cx_s.at[e, g, b], cx_r.at[e, g, b], device_id={"col": target}, device_id_type=MESH)
+        for e in range(2):
+            @pl.when(z == (0 if e == 0 else n - 1))
+            def _():
+                for b in range(blocks):
+                    @pl.when(i == ready + b)
+                    def _():
+                        attend(e, 0, b)
+
+        return carry
+
+    lax.fori_loop(0, max(pieces + SKEW * (n - 1), ready + blocks), step, 0)
 
     for e in range(2):
         @pl.when(z == (0 if e == 0 else n - 1))
         def _():
             def group(g, carry):
                 for b in range(blocks):
-                    first, last = b * qb, (b + 1) * qb
-                    for h in range(0, wg, HD):
-                        ctx[e, g, first:last, h : h + HD] = attend_block(
-                            final[g, 0, first:last, h : h + HD], final[g, 1, :last, h : h + HD],
-                            final[g, 2, :last, h : h + HD], first)
-                    ctx_copy(e, g, b).start()
+                    attend(e, g, b)
                 return carry
 
-            lax.fori_loop(0, groups, group, 0)
+            lax.fori_loop(1, groups, group, 0)
 
     def relay(i, carry):
         g, b = i // blocks, lax.rem(i, blocks)

time: 215 us -> 202 us (0.940)
  Pallas kernels: 213 us -> 200 us
    pallas_call x1, Pallas kernels: 213 us -> 200 us  [fused_local(): pl.pallas_call(partial(fused_kernel, n, ranks), in_specs=[pl.BlockSpec(me...]
where the time goes in v2:
time: 202 us
  Pallas kernels  200 us (99%)
  local copies, waits for them, and re-layouts  2.06 us (1%)
    pallas_call x1, Pallas kernels, fused_local(): pl.pallas_call(partial(fused_kernel, n, ranks), in_specs=[pl.BlockSpec(me...  200 us

profile of v2, /device:TPU:0, one launch (start us, length us, event | category | flops | bytes accessed | tf_op | source)
XLA Modules:
  0.0 202.0 jit_solution(14072161305341572038)
XLA Ops:
  0.0 199.9 %shard_map.37 = bf16[128,3072]{1,0:T(8,128)(2,1)} custom-call(bf16[128,3072]{1,0:T(8,128)(2,1)} %tok_ref.1, bf16[3,3072,1024]{2,1,0:T(8,128)(2,1)} %bitcast.1, bf16[1024,3072]{1,0:T(8,128)(2,1)} %ow_ref.1), custom_call_target="tpu_custom_call" | custom-call | tf_op jit(solution)/shard_map/pallas_call | solution.py:359
  199.9 2.1 %copy.5 = bf16[128,3072]{1,0:T(8,128)(2,1)} copy(bf16[128,3072]{1,0:T(8,128)(2,1)} %shard_map.37) | data formatting | bytes 1572864
